TPU v7x, 256 devices: a whole 4x4x8 slice. The times are simulated.
256 devices in a mesh: area: 32 (over y, x, core), pop: 8 (over z).
Axes of the slice: x: 4, y: 4, z: 8, core: 2. Of those that a mesh axis runs over, the one named last changes fastest.
Arguments:
- history: bfloat16 [4, 32, 64, 32, 128], P(None, 'area', 'pop'), may hold values from -1 to 1
- external: bfloat16 [32, 64, 32, 128], P('area', 'pop'), may hold values from -6 to 6
- leak_rate: float32 [32, 64, 128], P('area', 'pop'), may hold values from 0.05 to 1
- intra_index: int32 [32, 64, 32], P('area', 'pop'), may hold values from 0 to 63
- intra_weight: bfloat16 [32, 64, 32, 128, 128], P('area', 'pop'), may hold values from -0.09375 to 0.09375
- inter_pick: int32 [32, 64, 12], P('area', 'pop'), may hold values from 0 to 1
- inter_weight: bfloat16 [32, 64, 12, 128, 128], P('area', 'pop'), may hold values from -0.15625 to 0.15625
- source_area: int32 [32, 12], replicated, may hold values from 0 to 31, as said below
- delays: int32 [32, 12], replicated, may hold values from 1 to 3
- live_blocks: int32 [32], replicated, may hold values from 8 to 64, as said below
Outputs:
- activity: float32 [32, 64, 32, 128], P('area', 'pop')
Inputs may be any that keep to these rules, and one draw needn't show every extreme that they name: `source_area`: the 12 source areas of an area are distinct and differ from the area itself. `live_blocks`: some area is fully populated and some has 8 populated blocks.
All inputs are finite; a program needn't handle non-finite values.
Results may differ from a plain program's by a relative error of at most 0.0014.
Values may be sent and summed in bfloat16 or wider, within the bound.
No kernel may reach another device: no remote copies, remote signals or barrier semaphores. Data moves between devices by JAX's collectives and lax.ppermute only.
A program may use at most 64 MiB of HBM per device.

v0:
```python
import jax
import jax.numpy as jnp
from jax import lax
from jax.sharding import PartitionSpec as P

SEND_DEV = 2
STEPS = 10


def shards(
    history,
    external,
    leak_rate,
    intra_index,
    intra_weight,
    inter_pick,
    inter_weight,
    source_area,
    delays,
    live_blocks,
):
    area_pos = lax.axis_index("area")
    pop_pos = lax.axis_index("pop")
    blk_local = history.shape[2]
    edge_count = inter_pick.shape[2]
    block_ids = pop_pos * blk_local + jnp.arange(blk_local, dtype=jnp.int32)
    alive_mask = (block_ids < live_blocks[area_pos]).astype(jnp.float32)[:, None, None]
    own_hist = (history[:, 0].astype(jnp.float32) * alive_mask[None]).astype(jnp.bfloat16)
    activity = own_hist[0].astype(jnp.float32)
    my_source = source_area[area_pos]
    tile_index = intra_index[0]
    w_inner = intra_weight[0]
    w_outer = inter_weight[0]
    flat_pick = jnp.arange(edge_count, dtype=jnp.int32)[None, :] * SEND_DEV + inter_pick[0]
    leak_cells = leak_rate[0][:, None, :]
    drive_ext = external[0].astype(jnp.float32)

    def advance(activity, rate_now, edge_rows):
        area_rates = lax.all_gather(rate_now, "pop", axis=0, tiled=True)
        tile_rows = jnp.take(area_rates, tile_index, axis=0)
        inner_term = jnp.einsum(
            "rkji,rktj->rti", w_inner, tile_rows, preferred_element_type=jnp.float32
        )
        flat_rows = edge_rows.reshape((edge_count * SEND_DEV,) + edge_rows.shape[2:])
        source_rows = jnp.take(flat_rows, flat_pick, axis=0)
        outer_term = jnp.einsum(
            "rkji,rktj->rti", w_outer, source_rows, preferred_element_type=jnp.float32
        )
        drive_term = jnp.tanh(inner_term + outer_term + drive_ext)
        return alive_mask * ((1.0 - leak_cells) * activity + leak_cells * drive_term)

    delay_to = jnp.sum(jnp.where(source_area == area_pos, delays, 0), axis=1)
    edge_flag = (delay_to > 0).astype(jnp.bfloat16)[:, None, None, None]

    def turn_slots(position, carried):
        activity, sent_hist, rate_now = carried
        chosen = jnp.take(sent_hist, delay_to, axis=0) * edge_flag
        received = lax.all_to_all(chosen, "area", split_axis=0, concat_axis=0, tiled=True)
        edge_rows = jnp.take(received, my_source, axis=0)
        activity = advance(activity, rate_now, edge_rows)
        rate_now = activity.astype(jnp.bfloat16)
        sent_hist = jnp.concatenate([rate_now[None, :SEND_DEV], sent_hist[:-1]], 0)
        return (activity, sent_hist, rate_now)

    activity, sent_hist, rate_now = lax.fori_loop(
        0, STEPS, turn_slots, (activity, own_hist[:, :SEND_DEV], own_hist[0])
    )
    return activity[None]


def solution(mesh):
    placed = (
        P(None, "area", "pop", None, None),
        P("area", "pop", None, None),
        P("area", "pop", None),
        P("area", "pop", None),
        P("area", "pop", None, None, None),
        P("area", "pop", None),
        P("area", "pop", None, None, None),
        P(),
        P(),
        P(),
    )
    return jax.shard_map(
        shards, mesh=mesh, in_specs=placed, out_specs=P("area", "pop", None, None), check_vma=False
    )
```

profile of v0, /device:TPU:4, one launch (start us, length us, event | category | flops | bytes accessed | tf_op | source)
XLA Modules:
  0.0 475.0 jit_solution(8111666128941133246)
XLA Ops:
  0.0 1.3 dynamic_slice.6
  1.9 1.1 fusion.23
  3.0 1.5 slice_bitcast_fusion.1
  6.8 467.5 %while.15 = (s32[]{:T(128)}, f32[8,32,128]{2,1,0:T(8,128)S(1)}, bf16[4,2,32,128]{3,2,1,0:T(8,128)(2,1)S(1)}, bf16[8,32,128]{2,1,0:T(8,128)(2,1)}, f32[8,1,128]{2...) while((s32[]{:T(128)}, f32[8,32,128]{2,1,0:T(8,128)S(1)}, ...), condition=%wide.region_2.3_spmd.clone, body=%wide.region_1.2_spmd.clone.sunk | while | flops 371433984 | bytes 26279644 | solution.py:65
  8.5 7.6 %all-to-all-start = ((bf16[32,2,32,128]{3,2,1,0:T(8,128)(2,1)}), bf16[32,2,32,128]{3,2,1,0:T(8,128)(2,1)S(1)}, u32[]{:S(2)}, u32[]{:S(2)}) async-start(bf16[32,2,32,128]{3,2,1,0:T(8,128)(2,1)} %select_multiply_fusion.2), calls=%async_computation | async-start | bytes 1048576 | tf_op jit(solution)/shard_map/while/body/eval_jaxpr/all_to_all | solution.py:58
  16.2 29.3 %all_gather.5 = bf16[64,32,128]{2,1,0:T(8,128)(2,1)S(1)} all-gather(bf16[8,32,128]{2,1,0:T(8,128)(2,1)} %get-tuple-element.261), channel_id=1, replica_groups=mesh['area'=32,'pop'=8] {'pop'}, dimensions={0}, use_global_device_ids=true | all-gather | bytes 589824 | tf_op jit(solution)/shard_map/while/body/eval_jaxpr/all_gather | solution.py:39
  45.8 1.0 gather_fusion
  47.4 4.3 fusion.40
  53.2 3.2 fusion.44
  58.8 7.2 %all-to-all-start = ((bf16[32,2,32,128]{3,2,1,0:T(8,128)(2,1)}), bf16[32,2,32,128]{3,2,1,0:T(8,128)(2,1)S(1)}, u32[]{:S(2)}, u32[]{:S(2)}) async-start(bf16[32,2,32,128]{3,2,1,0:T(8,128)(2,1)} %select_multiply_fusion.2), calls=%async_computation | async-start | bytes 1048576 | tf_op jit(solution)/shard_map/while/body/eval_jaxpr/all_to_all | solution.py:58
  66.1 25.6 %all_gather.5 = bf16[64,32,128]{2,1,0:T(8,128)(2,1)S(1)} all-gather(bf16[8,32,128]{2,1,0:T(8,128)(2,1)} %get-tuple-element.261), channel_id=1, replica_groups=mesh['area'=32,'pop'=8] {'pop'}, dimensions={0}, use_global_device_ids=true | all-gather | bytes 589824 | tf_op jit(solution)/shard_map/while/body/eval_jaxpr/all_gather | solution.py:39
  93.7 4.3 fusion.40
  99.5 3.2 fusion.44
  105.1 7.3 %all-to-all-start = ((bf16[32,2,32,128]{3,2,1,0:T(8,128)(2,1)}), bf16[32,2,32,128]{3,2,1,0:T(8,128)(2,1)S(1)}, u32[]{:S(2)}, u32[]{:S(2)}) async-start(bf16[32,2,32,128]{3,2,1,0:T(8,128)(2,1)} %select_multiply_fusion.2), calls=%async_computation | async-start | bytes 1048576 | tf_op jit(solution)/shard_map/while/body/eval_jaxpr/all_to_all | solution.py:58
  112.5 25.6 %all_gather.5 = bf16[64,32,128]{2,1,0:T(8,128)(2,1)S(1)} all-gather(bf16[8,32,128]{2,1,0:T(8,128)(2,1)} %get-tuple-element.261), channel_id=1, replica_groups=mesh['area'=32,'pop'=8] {'pop'}, dimensions={0}, use_global_device_ids=true | all-gather | bytes 589824 | tf_op jit(solution)/shard_map/while/body/eval_jaxpr/all_gather | solution.py:39
  138.5 1.0 gather_fusion
  140.1 4.3 fusion.40
  145.9 3.2 fusion.44
  151.5 7.3 %all-to-all-start = ((bf16[32,2,32,128]{3,2,1,0:T(8,128)(2,1)}), bf16[32,2,32,128]{3,2,1,0:T(8,128)(2,1)S(1)}, u32[]{:S(2)}, u32[]{:S(2)}) async-start(bf16[32,2,32,128]{3,2,1,0:T(8,128)(2,1)} %select_multiply_fusion.2), calls=%async_computation | async-start | bytes 1048576 | tf_op jit(solution)/shard_map/while/body/eval_jaxpr/all_to_all | solution.py:58
  158.9 25.6 %all_gather.5 = bf16[64,32,128]{2,1,0:T(8,128)(2,1)S(1)} all-gather(bf16[8,32,128]{2,1,0:T(8,128)(2,1)} %get-tuple-element.261), channel_id=1, replica_groups=mesh['area'=32,'pop'=8] {'pop'}, dimensions={0}, use_global_device_ids=true | all-gather | bytes 589824 | tf_op jit(solution)/shard_map/while/body/eval_jaxpr/all_gather | solution.py:39
  186.5 4.3 fusion.40
  192.3 3.2 fusion.44
  197.9 7.3 %all-to-all-start = ((bf16[32,2,32,128]{3,2,1,0:T(8,128)(2,1)}), bf16[32,2,32,128]{3,2,1,0:T(8,128)(2,1)S(1)}, u32[]{:S(2)}, u32[]{:S(2)}) async-start(bf16[32,2,32,128]{3,2,1,0:T(8,128)(2,1)} %select_multiply_fusion.2), calls=%async_computation | async-start | bytes 1048576 | tf_op jit(solution)/shard_map/while/body/eval_jaxpr/all_to_all | solution.py:58
  205.2 25.6 %all_gather.5 = bf16[64,32,128]{2,1,0:T(8,128)(2,1)S(1)} all-gather(bf16[8,32,128]{2,1,0:T(8,128)(2,1)} %get-tuple-element.261), channel_id=1, replica_groups=mesh['area'=32,'pop'=8] {'pop'}, dimensions={0}, use_global_device_ids=true | all-gather | bytes 589824 | tf_op jit(solution)/shard_map/while/body/eval_jaxpr/all_gather | solution.py:39
  231.3 1.0 gather_fusion
  232.9 4.3 fusion.40
  238.6 3.2 fusion.44
  244.2 7.2 %all-to-all-start = ((bf16[32,2,32,128]{3,2,1,0:T(8,128)(2,1)}), bf16[32,2,32,128]{3,2,1,0:T(8,128)(2,1)S(1)}, u32[]{:S(2)}, u32[]{:S(2)}) async-start(bf16[32,2,32,128]{3,2,1,0:T(8,128)(2,1)} %select_multiply_fusion.2), calls=%async_computation | async-start | bytes 1048576 | tf_op jit(solution)/shard_map/while/body/eval_jaxpr/all_to_all | solution.py:58
  251.6 25.6 %all_gather.5 = bf16[64,32,128]{2,1,0:T(8,128)(2,1)S(1)} all-gather(bf16[8,32,128]{2,1,0:T(8,128)(2,1)} %get-tuple-element.261), channel_id=1, replica_groups=mesh['area'=32,'pop'=8] {'pop'}, dimensions={0}, use_global_device_ids=true | all-gather | bytes 589824 | tf_op jit(solution)/shard_map/while/body/eval_jaxpr/all_gather | solution.py:39
  277.6 1.0 gather_fusion
  279.2 4.3 fusion.40
  285.0 3.2 fusion.44
  290.6 7.2 %all-to-all-start = ((bf16[32,2,32,128]{3,2,1,0:T(8,128)(2,1)}), bf16[32,2,32,128]{3,2,1,0:T(8,128)(2,1)S(1)}, u32[]{:S(2)}, u32[]{:S(2)}) async-start(bf16[32,2,32,128]{3,2,1,0:T(8,128)(2,1)} %select_multiply_fusion.2), calls=%async_computation | async-start | bytes 1048576 | tf_op jit(solution)/shard_map/while/body/eval_jaxpr/all_to_all | solution.py:58
  297.9 25.7 %all_gather.5 = bf16[64,32,128]{2,1,0:T(8,128)(2,1)S(1)} all-gather(bf16[8,32,128]{2,1,0:T(8,128)(2,1)} %get-tuple-element.261), channel_id=1, replica_groups=mesh['area'=32,'pop'=8] {'pop'}, dimensions={0}, use_global_device_ids=true | all-gather | bytes 589824 | tf_op jit(solution)/shard_map/while/body/eval_jaxpr/all_gather | solution.py:39
  325.6 4.3 fusion.40
  331.3 3.2 fusion.44
  337.0 7.2 %all-to-all-start = ((bf16[32,2,32,128]{3,2,1,0:T(8,128)(2,1)}), bf16[32,2,32,128]{3,2,1,0:T(8,128)(2,1)S(1)}, u32[]{:S(2)}, u32[]{:S(2)}) async-start(bf16[32,2,32,128]{3,2,1,0:T(8,128)(2,1)} %select_multiply_fusion.2), calls=%async_computation | async-start | bytes 1048576 | tf_op jit(solution)/shard_map/while/body/eval_jaxpr/all_to_all | solution.py:58
  344.3 25.7 %all_gather.5 = bf16[64,32,128]{2,1,0:T(8,128)(2,1)S(1)} all-gather(bf16[8,32,128]{2,1,0:T(8,128)(2,1)} %get-tuple-element.261), channel_id=1, replica_groups=mesh['area'=32,'pop'=8] {'pop'}, dimensions={0}, use_global_device_ids=true | all-gather | bytes 589824 | tf_op jit(solution)/shard_map/while/body/eval_jaxpr/all_gather | solution.py:39
  371.9 4.3 fusion.40
  377.7 3.2 fusion.44
  383.3 7.2 %all-to-all-start = ((bf16[32,2,32,128]{3,2,1,0:T(8,128)(2,1)}), bf16[32,2,32,128]{3,2,1,0:T(8,128)(2,1)S(1)}, u32[]{:S(2)}, u32[]{:S(2)}) async-start(bf16[32,2,32,128]{3,2,1,0:T(8,128)(2,1)} %select_multiply_fusion.2), calls=%async_computation | async-start | bytes 1048576 | tf_op jit(solution)/shard_map/while/body/eval_jaxpr/all_to_all | solution.py:58
  390.6 25.7 %all_gather.5 = bf16[64,32,128]{2,1,0:T(8,128)(2,1)S(1)} all-gather(bf16[8,32,128]{2,1,0:T(8,128)(2,1)} %get-tuple-element.261), channel_id=1, replica_groups=mesh['area'=32,'pop'=8] {'pop'}, dimensions={0}, use_global_device_ids=true | all-gather | bytes 589824 | tf_op jit(solution)/shard_map/while/body/eval_jaxpr/all_gather | solution.py:39
  418.3 4.3 fusion.40
  424.0 3.2 fusion.44
  429.6 7.2 %all-to-all-start = ((bf16[32,2,32,128]{3,2,1,0:T(8,128)(2,1)}), bf16[32,2,32,128]{3,2,1,0:T(8,128)(2,1)S(1)}, u32[]{:S(2)}, u32[]{:S(2)}) async-start(bf16[32,2,32,128]{3,2,1,0:T(8,128)(2,1)} %select_multiply_fusion.2), calls=%async_computation | async-start | bytes 1048576 | tf_op jit(solution)/shard_map/while/body/eval_jaxpr/all_to_all | solution.py:58
  436.9 25.7 %all_gather.5 = bf16[64,32,128]{2,1,0:T(8,128)(2,1)S(1)} all-gather(bf16[8,32,128]{2,1,0:T(8,128)(2,1)} %get-tuple-element.261), channel_id=1, replica_groups=mesh['area'=32,'pop'=8] {'pop'}, dimensions={0}, use_global_device_ids=true | all-gather | bytes 589824 | tf_op jit(solution)/shard_map/while/body/eval_jaxpr/all_gather | solution.py:39
  464.6 4.3 fusion.40
  470.3 3.2 fusion.44
  (325 shorter events, 56.9 us)
Async XLA Ops:
  6.8 9.3 %copy-start.1 = (s32[8,32]{1,0:T(8,128)S(1)}, s32[8,32]{1,0:T(8,128)}, u32[]{:S(2)}) copy-start(s32[8,32]{1,0:T(8,128)} %get-tuple-element.279) | copy-start | bytes 3076 | tf_op jit(solution)/shard_map/while
  6.8 39.0 %copy-start.2 = (f32[8,1,128]{2,0,1:T(8,128)S(1)}, f32[8,1,128]{2,0,1:T(8,128)}, u32[]{:S(2)}) copy-start(f32[8,1,128]{2,0,1:T(8,128)} %get-tuple-element.278) | copy-start | bytes 12292 | tf_op jit(solution)/shard_map/while
  8.5 43.3 %all-to-all-start = ((bf16[32,2,32,128]{3,2,1,0:T(8,128)(2,1)}), bf16[32,2,32,128]{3,2,1,0:T(8,128)(2,1)S(1)}, u32[]{:S(2)}, u32[]{:S(2)}) async-start(bf16[32,2,32,128]{3,2,1,0:T(8,128)(2,1)} %select_multiply_fusion.2), calls=%async_computation | async-start | bytes 1048576 | tf_op jit(solution)/shard_map/while/body/eval_jaxpr/all_to_all | solution.py:58
  57.1 8.9 %copy-start.1 = (s32[8,32]{1,0:T(8,128)S(1)}, s32[8,32]{1,0:T(8,128)}, u32[]{:S(2)}) copy-start(s32[8,32]{1,0:T(8,128)} %get-tuple-element.279) | copy-start | bytes 3076 | tf_op jit(solution)/shard_map/while
  57.1 34.9 %copy-start.2 = (f32[8,1,128]{2,0,1:T(8,128)S(1)}, f32[8,1,128]{2,0,1:T(8,128)}, u32[]{:S(2)}) copy-start(f32[8,1,128]{2,0,1:T(8,128)} %get-tuple-element.278) | copy-start | bytes 12292 | tf_op jit(solution)/shard_map/while
  58.8 39.3 %all-to-all-start = ((bf16[32,2,32,128]{3,2,1,0:T(8,128)(2,1)}), bf16[32,2,32,128]{3,2,1,0:T(8,128)(2,1)S(1)}, u32[]{:S(2)}, u32[]{:S(2)}) async-start(bf16[32,2,32,128]{3,2,1,0:T(8,128)(2,1)} %select_multiply_fusion.2), calls=%async_computation | async-start | bytes 1048576 | tf_op jit(solution)/shard_map/while/body/eval_jaxpr/all_to_all | solution.py:58
  103.4 9.0 %copy-start.1 = (s32[8,32]{1,0:T(8,128)S(1)}, s32[8,32]{1,0:T(8,128)}, u32[]{:S(2)}) copy-start(s32[8,32]{1,0:T(8,128)} %get-tuple-element.279) | copy-start | bytes 3076 | tf_op jit(solution)/shard_map/while
  103.5 35.0 %copy-start.2 = (f32[8,1,128]{2,0,1:T(8,128)S(1)}, f32[8,1,128]{2,0,1:T(8,128)}, u32[]{:S(2)}) copy-start(f32[8,1,128]{2,0,1:T(8,128)} %get-tuple-element.278) | copy-start | bytes 12292 | tf_op jit(solution)/shard_map/while
  105.1 39.4 %all-to-all-start = ((bf16[32,2,32,128]{3,2,1,0:T(8,128)(2,1)}), bf16[32,2,32,128]{3,2,1,0:T(8,128)(2,1)S(1)}, u32[]{:S(2)}, u32[]{:S(2)}) async-start(bf16[32,2,32,128]{3,2,1,0:T(8,128)(2,1)} %select_multiply_fusion.2), calls=%async_computation | async-start | bytes 1048576 | tf_op jit(solution)/shard_map/while/body/eval_jaxpr/all_to_all | solution.py:58
  149.8 9.0 %copy-start.1 = (s32[8,32]{1,0:T(8,128)S(1)}, s32[8,32]{1,0:T(8,128)}, u32[]{:S(2)}) copy-start(s32[8,32]{1,0:T(8,128)} %get-tuple-element.279) | copy-start | bytes 3076 | tf_op jit(solution)/shard_map/while
  149.8 35.0 %copy-start.2 = (f32[8,1,128]{2,0,1:T(8,128)S(1)}, f32[8,1,128]{2,0,1:T(8,128)}, u32[]{:S(2)}) copy-start(f32[8,1,128]{2,0,1:T(8,128)} %get-tuple-element.278) | copy-start | bytes 12292 | tf_op jit(solution)/shard_map/while
  151.5 39.4 %all-to-all-start = ((bf16[32,2,32,128]{3,2,1,0:T(8,128)(2,1)}), bf16[32,2,32,128]{3,2,1,0:T(8,128)(2,1)S(1)}, u32[]{:S(2)}, u32[]{:S(2)}) async-start(bf16[32,2,32,128]{3,2,1,0:T(8,128)(2,1)} %select_multiply_fusion.2), calls=%async_computation | async-start | bytes 1048576 | tf_op jit(solution)/shard_map/while/body/eval_jaxpr/all_to_all | solution.py:58
  196.2 8.9 %copy-start.1 = (s32[8,32]{1,0:T(8,128)S(1)}, s32[8,32]{1,0:T(8,128)}, u32[]{:S(2)}) copy-start(s32[8,32]{1,0:T(8,128)} %get-tuple-element.279) | copy-start | bytes 3076 | tf_op jit(solution)/shard_map/while
  196.2 35.0 %copy-start.2 = (f32[8,1,128]{2,0,1:T(8,128)S(1)}, f32[8,1,128]{2,0,1:T(8,128)}, u32[]{:S(2)}) copy-start(f32[8,1,128]{2,0,1:T(8,128)} %get-tuple-element.278) | copy-start | bytes 12292 | tf_op jit(solution)/shard_map/while
  197.9 39.3 %all-to-all-start = ((bf16[32,2,32,128]{3,2,1,0:T(8,128)(2,1)}), bf16[32,2,32,128]{3,2,1,0:T(8,128)(2,1)S(1)}, u32[]{:S(2)}, u32[]{:S(2)}) async-start(bf16[32,2,32,128]{3,2,1,0:T(8,128)(2,1)} %select_multiply_fusion.2), calls=%async_computation | async-start | bytes 1048576 | tf_op jit(solution)/shard_map/while/body/eval_jaxpr/all_to_all | solution.py:58
  242.6 8.9 %copy-start.1 = (s32[8,32]{1,0:T(8,128)S(1)}, s32[8,32]{1,0:T(8,128)}, u32[]{:S(2)}) copy-start(s32[8,32]{1,0:T(8,128)} %get-tuple-element.279) | copy-start | bytes 3076 | tf_op jit(solution)/shard_map/while
  242.6 35.0 %copy-start.2 = (f32[8,1,128]{2,0,1:T(8,128)S(1)}, f32[8,1,128]{2,0,1:T(8,128)}, u32[]{:S(2)}) copy-start(f32[8,1,128]{2,0,1:T(8,128)} %get-tuple-element.278) | copy-start | bytes 12292 | tf_op jit(solution)/shard_map/while
  244.2 39.3 %all-to-all-start = ((bf16[32,2,32,128]{3,2,1,0:T(8,128)(2,1)}), bf16[32,2,32,128]{3,2,1,0:T(8,128)(2,1)S(1)}, u32[]{:S(2)}, u32[]{:S(2)}) async-start(bf16[32,2,32,128]{3,2,1,0:T(8,128)(2,1)} %select_multiply_fusion.2), calls=%async_computation | async-start | bytes 1048576 | tf_op jit(solution)/shard_map/while/body/eval_jaxpr/all_to_all | solution.py:58
  289.0 8.9 %copy-start.1 = (s32[8,32]{1,0:T(8,128)S(1)}, s32[8,32]{1,0:T(8,128)}, u32[]{:S(2)}) copy-start(s32[8,32]{1,0:T(8,128)} %get-tuple-element.279) | copy-start | bytes 3076 | tf_op jit(solution)/shard_map/while
  289.0 35.0 %copy-start.2 = (f32[8,1,128]{2,0,1:T(8,128)S(1)}, f32[8,1,128]{2,0,1:T(8,128)}, u32[]{:S(2)}) copy-start(f32[8,1,128]{2,0,1:T(8,128)} %get-tuple-element.278) | copy-start | bytes 12292 | tf_op jit(solution)/shard_map/while
  290.6 39.3 %all-to-all-start = ((bf16[32,2,32,128]{3,2,1,0:T(8,128)(2,1)}), bf16[32,2,32,128]{3,2,1,0:T(8,128)(2,1)S(1)}, u32[]{:S(2)}, u32[]{:S(2)}) async-start(bf16[32,2,32,128]{3,2,1,0:T(8,128)(2,1)} %select_multiply_fusion.2), calls=%async_computation | async-start | bytes 1048576 | tf_op jit(solution)/shard_map/while/body/eval_jaxpr/all_to_all | solution.py:58
  335.3 8.9 %copy-start.1 = (s32[8,32]{1,0:T(8,128)S(1)}, s32[8,32]{1,0:T(8,128)}, u32[]{:S(2)}) copy-start(s32[8,32]{1,0:T(8,128)} %get-tuple-element.279) | copy-start | bytes 3076 | tf_op jit(solution)/shard_map/while
  335.3 35.0 %copy-start.2 = (f32[8,1,128]{2,0,1:T(8,128)S(1)}, f32[8,1,128]{2,0,1:T(8,128)}, u32[]{:S(2)}) copy-start(f32[8,1,128]{2,0,1:T(8,128)} %get-tuple-element.278) | copy-start | bytes 12292 | tf_op jit(solution)/shard_map/while
  337.0 39.3 %all-to-all-start = ((bf16[32,2,32,128]{3,2,1,0:T(8,128)(2,1)}), bf16[32,2,32,128]{3,2,1,0:T(8,128)(2,1)S(1)}, u32[]{:S(2)}, u32[]{:S(2)}) async-start(bf16[32,2,32,128]{3,2,1,0:T(8,128)(2,1)} %select_multiply_fusion.2), calls=%async_computation | async-start | bytes 1048576 | tf_op jit(solution)/shard_map/while/body/eval_jaxpr/all_to_all | solution.py:58
  381.6 8.9 %copy-start.1 = (s32[8,32]{1,0:T(8,128)S(1)}, s32[8,32]{1,0:T(8,128)}, u32[]{:S(2)}) copy-start(s32[8,32]{1,0:T(8,128)} %get-tuple-element.279) | copy-start | bytes 3076 | tf_op jit(solution)/shard_map/while
  381.6 35.0 %copy-start.2 = (f32[8,1,128]{2,0,1:T(8,128)S(1)}, f32[8,1,128]{2,0,1:T(8,128)}, u32[]{:S(2)}) copy-start(f32[8,1,128]{2,0,1:T(8,128)} %get-tuple-element.278) | copy-start | bytes 12292 | tf_op jit(solution)/shard_map/while
  383.3 39.3 %all-to-all-start = ((bf16[32,2,32,128]{3,2,1,0:T(8,128)(2,1)}), bf16[32,2,32,128]{3,2,1,0:T(8,128)(2,1)S(1)}, u32[]{:S(2)}, u32[]{:S(2)}) async-start(bf16[32,2,32,128]{3,2,1,0:T(8,128)(2,1)} %select_multiply_fusion.2), calls=%async_computation | async-start | bytes 1048576 | tf_op jit(solution)/shard_map/while/body/eval_jaxpr/all_to_all | solution.py:58
  428.0 8.9 %copy-start.1 = (s32[8,32]{1,0:T(8,128)S(1)}, s32[8,32]{1,0:T(8,128)}, u32[]{:S(2)}) copy-start(s32[8,32]{1,0:T(8,128)} %get-tuple-element.279) | copy-start | bytes 3076 | tf_op jit(solution)/shard_map/while
  428.0 35.0 %copy-start.2 = (f32[8,1,128]{2,0,1:T(8,128)S(1)}, f32[8,1,128]{2,0,1:T(8,128)}, u32[]{:S(2)}) copy-start(f32[8,1,128]{2,0,1:T(8,128)} %get-tuple-element.278) | copy-start | bytes 12292 | tf_op jit(solution)/shard_map/while
  429.6 39.3 %all-to-all-start = ((bf16[32,2,32,128]{3,2,1,0:T(8,128)(2,1)}), bf16[32,2,32,128]{3,2,1,0:T(8,128)(2,1)S(1)}, u32[]{:S(2)}, u32[]{:S(2)}) async-start(bf16[32,2,32,128]{3,2,1,0:T(8,128)(2,1)} %select_multiply_fusion.2), calls=%async_computation | async-start | bytes 1048576 | tf_op jit(solution)/shard_map/while/body/eval_jaxpr/all_to_all | solution.py:58
  474.3 0.7 copy-start
where the time goes:
time: 478 us; the launch traced here: 475 us
  blocking collectives  260 us (54%)
  matrix products  75.3 us (16%)
  starting transfers between devices  72.8 us (15%)
  local copies, waits for them, and re-layouts  42.8 us (9%)
  other arithmetic  21.9 us (5%)
    all_gather x10, blocking collectives, advance(): area_rates = lax.all_gather(rate_now, 'pop', axis=0, tiled=True)  260 us
    all_to_all x10, starting transfers between devices, turn_slots(): lax.all_to_all(chosen, 'area', split_axis=0, concat_axis=0, tiled=True)  72.8 us
    dot_general x10, matrix products, advance(): jnp.einsum('rkji,rktj->rti', w_inner, tile_rows, preferred_element_type=j...  43.2 us
    dot_general x10, matrix products, advance(): jnp.einsum('rkji,rktj->rti', w_outer, source_rows, preferred_element_type...  32.1 us
    gather x10, local copies, waits for them, and re-layouts, advance(): tile_rows = jnp.take(area_rates, tile_index, axis=0)  9.94 us
  transfers between devices with their start and end apart: 10, of which 0 were waited for; matrix products, arithmetic and copies ran while one was open for 13% of the time, Pallas kernels for 0%

commit v1 on v0

--- a/solution.py
+++ b/solution.py
@@ -36,7 +36,9 @@
     drive_ext = external[0].astype(jnp.float32)
 
     def advance(activity, rate_now, edge_rows):
-        area_rates = lax.all_gather(rate_now, "pop", axis=0, tiled=True)
+        area_rates = jnp.concatenate(
+            lax.all_to_all(jnp.stack([rate_now] * lax.axis_size("pop")), "pop", 0, 0), axis=0
+        )
         tile_rows = jnp.take(area_rates, tile_index, axis=0)
         inner_term = jnp.einsum(
             "rkji,rktj->rti", w_inner, tile_rows, preferred_element_type=jnp.float32

time: 478 us -> 483 us (1.010)
  blocking collectives: 260 us -> 0 us
  waiting for transfers between devices: 0.03 us -> 247 us
  starting transfers between devices: 72.8 us -> 104 us
  matrix products: 75.3 us -> 51.3 us
  local copies, waits for them, and re-layouts: 42.8 us -> 50.1 us
    all_gather x10 -> x0, blocking collectives: 260 us -> none  [advance(): area_rates = lax.all_gather(rate_now, 'pop', axis=0, tiled=True)]
    all_to_all x0 -> x10, waiting for transfers between devices: none -> 152 us  [advance(): lax.all_to_all(jnp.stack([rate_now] * lax.axis_size('pop')), 'pop', 0, 0)]
    all_to_all x10, waiting for transfers between devices: 0.03 us -> 95.1 us  [turn_slots(): lax.all_to_all(chosen, 'area', split_axis=0, concat_axis=0, tiled=True)]
    all_to_all x0 -> x10, starting transfers between devices: none -> 39.9 us  [advance(): lax.all_to_all(jnp.stack([rate_now] * lax.axis_size('pop')), 'pop', 0, 0)]
    dot_general x10, matrix products: 32.1 us -> 6.86 us  [advance(): jnp.einsum('rkji,rktj->rti', w_outer, source_rows, preferred_element_type...]
    another operation x0 -> x10, local copies, waits for them, and re-layouts: none -> 8.75 us  [advance(): jnp.stack([rate_now] * lax.axis_size('pop'))]
    all_to_all x10, starting transfers between devices: 72.8 us -> 64.2 us  [turn_slots(): lax.all_to_all(chosen, 'area', split_axis=0, concat_axis=0, tiled=True)]
    broadcast_in_dim x10, local copies, waits for them, and re-layouts: 7.18 us -> 0.03 us  [turn_slots(): sent_hist = jnp.concatenate([rate_now[None, :SEND_DEV], sent_hist[:-1]], 0)]
  transfers between devices with their start and end apart: 10 -> 20, of which waited for: 0 -> 20; matrix products, arithmetic and copies ran while one was open for 13% -> 5% of each run, Pallas kernels for 0% -> 0%
where the time goes in v1:
time: 483 us; the launch traced here: 477 us
  waiting for transfers between devices  247 us (51%)
  starting transfers between devices  104 us (22%)
  matrix products  51.3 us (11%)
  local copies, waits for them, and re-layouts  50.1 us (10%)
  other arithmetic  22.1 us (5%)
    all_to_all x10, waiting for transfers between devices, advance(): lax.all_to_all(jnp.stack([rate_now] * lax.axis_size('pop')), 'pop', 0, 0)  152 us
    all_to_all x10, waiting for transfers between devices, turn_slots(): lax.all_to_all(chosen, 'area', split_axis=0, concat_axis=0, tiled=True)  95.1 us
    all_to_all x10, starting transfers between devices, turn_slots(): lax.all_to_all(chosen, 'area', split_axis=0, concat_axis=0, tiled=True)  64.2 us
    dot_general x10, matrix products, advance(): jnp.einsum('rkji,rktj->rti', w_inner, tile_rows, preferred_element_type=j...  44.5 us
    all_to_all x10, starting transfers between devices, advance(): lax.all_to_all(jnp.stack([rate_now] * lax.axis_size('pop')), 'pop', 0, 0)  39.9 us
    gather x10, local copies, waits for them, and re-layouts, advance(): tile_rows = jnp.take(area_rates, tile_index, axis=0)  9.93 us
  transfers between devices with their start and end apart: 20, of which 20 were waited for; matrix products, arithmetic and copies ran while one was open for 5% of the time, Pallas kernels for 0%

profile of v1, /device:TPU:4, one launch (start us, length us, event | category | flops | bytes accessed | tf_op | source)
XLA Modules:
  0.0 477.4 jit_solution(3095026721901738118)
XLA Ops:
  6.9 470.4 %while.15 = (s32[]{:T(128)}, f32[8,32,128]{2,1,0:T(8,128)}, bf16[4,2,32,128]{3,2,1,0:T(8,128)(2,1)S(1)}, bf16[8,32,128]{2,1,0:T(8,128)(2,1)S(1)}, f32[8,1,128]{2...) while((s32[]{:T(128)}, f32[8,32,128]{2,1,0:T(8,128)}, ...), condition=%wide.region_2.3_spmd.clone, body=%wide.region_1.2_spmd.clone.sunk | while | flops 371433984 | bytes 42008428 | solution.py:67
  8.6 7.6 %all-to-all-start.1 = ((bf16[32,2,32,128]{3,2,1,0:T(8,128)(2,1)}), bf16[32,2,32,128]{3,2,1,0:T(8,128)(2,1)S(1)}, u32[]{:S(2)}, u32[]{:S(2)}) async-start(bf16[32,2,32,128]{3,2,1,0:T(8,128)(2,1)} %select_multiply_fusion.2), calls=%async_computation.1 | async-start | bytes 1048576 | tf_op jit(solution)/shard_map/while/body/eval_jaxpr/all_to_all | solution.py:60
  16.4 9.4 %all-to-all-done.1 = bf16[32,2,32,128]{3,2,1,0:T(8,128)(2,1)S(1)} async-done(((bf16[32,2,32,128]{3,2,1,0:T(8,128)(2,1)}), bf16[32,2,32,128]{3,2,1,0:T(8,128)(2,1)S(1)}, u32[]{:S(2)}, u32[]{:S(2)}) %all-to-all-start.1) | async-done | bytes 524320 | tf_op jit(solution)/shard_map/while/body/eval_jaxpr/all_to_all | solution.py:60
  26.7 8.5 %all-to-all-start = ((bf16[8,8,32,128]{3,2,1,0:T(8,128)(2,1)}), bf16[8,8,32,128]{3,2,1,0:T(8,128)(2,1)S(1)}, u32[]{:S(2)}, u32[]{:S(2)}) async-start(bf16[8,8,32,128]{3,2,1,0:T(8,128)(2,1)} %stack.4), calls=%async_computation | async-start | bytes 1048576 | tf_op jit(solution)/shard_map/while/body/eval_jaxpr/all_to_all | solution.py:40
  37.5 15.0 %all-to-all-done = bf16[8,8,32,128]{3,2,1,0:T(8,128)(2,1)S(1)} async-done(((bf16[8,8,32,128]{3,2,1,0:T(8,128)(2,1)}), bf16[8,8,32,128]{3,2,1,0:T(8,128)(2,1)S(1)}, u32[]{:S(2)}, u32[]{:S(2)}) %all-to-all-start) | async-done | bytes 524320 | tf_op jit(solution)/shard_map/while/body/eval_jaxpr/all_to_all | solution.py:40
  53.5 4.4 fusion.40
  61.0 6.4 %all-to-all-start.1 = ((bf16[32,2,32,128]{3,2,1,0:T(8,128)(2,1)}), bf16[32,2,32,128]{3,2,1,0:T(8,128)(2,1)S(1)}, u32[]{:S(2)}, u32[]{:S(2)}) async-start(bf16[32,2,32,128]{3,2,1,0:T(8,128)(2,1)} %select_multiply_fusion.2), calls=%async_computation.1 | async-start | bytes 1048576 | tf_op jit(solution)/shard_map/while/body/eval_jaxpr/all_to_all | solution.py:60
  67.6 9.4 %all-to-all-done.1 = bf16[32,2,32,128]{3,2,1,0:T(8,128)(2,1)S(1)} async-done(((bf16[32,2,32,128]{3,2,1,0:T(8,128)(2,1)}), bf16[32,2,32,128]{3,2,1,0:T(8,128)(2,1)S(1)}, u32[]{:S(2)}, u32[]{:S(2)}) %all-to-all-start.1) | async-done | bytes 524320 | tf_op jit(solution)/shard_map/while/body/eval_jaxpr/all_to_all | solution.py:60
  77.9 3.5 all-to-all-start
  83.7 15.2 %all-to-all-done = bf16[8,8,32,128]{3,2,1,0:T(8,128)(2,1)S(1)} async-done(((bf16[8,8,32,128]{3,2,1,0:T(8,128)(2,1)}), bf16[8,8,32,128]{3,2,1,0:T(8,128)(2,1)S(1)}, u32[]{:S(2)}, u32[]{:S(2)}) %all-to-all-start) | async-done | bytes 524320 | tf_op jit(solution)/shard_map/while/body/eval_jaxpr/all_to_all | solution.py:40
  100.0 4.4 fusion.40
  107.4 6.3 %all-to-all-start.1 = ((bf16[32,2,32,128]{3,2,1,0:T(8,128)(2,1)}), bf16[32,2,32,128]{3,2,1,0:T(8,128)(2,1)S(1)}, u32[]{:S(2)}, u32[]{:S(2)}) async-start(bf16[32,2,32,128]{3,2,1,0:T(8,128)(2,1)} %select_multiply_fusion.2), calls=%async_computation.1 | async-start | bytes 1048576 | tf_op jit(solution)/shard_map/while/body/eval_jaxpr/all_to_all | solution.py:60
  114.0 9.5 %all-to-all-done.1 = bf16[32,2,32,128]{3,2,1,0:T(8,128)(2,1)S(1)} async-done(((bf16[32,2,32,128]{3,2,1,0:T(8,128)(2,1)}), bf16[32,2,32,128]{3,2,1,0:T(8,128)(2,1)S(1)}, u32[]{:S(2)}, u32[]{:S(2)}) %all-to-all-start.1) | async-done | bytes 524320 | tf_op jit(solution)/shard_map/while/body/eval_jaxpr/all_to_all | solution.py:60
  130.2 15.2 %all-to-all-done = bf16[8,8,32,128]{3,2,1,0:T(8,128)(2,1)S(1)} async-done(((bf16[8,8,32,128]{3,2,1,0:T(8,128)(2,1)}), bf16[8,8,32,128]{3,2,1,0:T(8,128)(2,1)S(1)}, u32[]{:S(2)}, u32[]{:S(2)}) %all-to-all-start) | async-done | bytes 524320 | tf_op jit(solution)/shard_map/while/body/eval_jaxpr/all_to_all | solution.py:40
  146.4 4.4 fusion.40
  153.9 6.3 %all-to-all-start.1 = ((bf16[32,2,32,128]{3,2,1,0:T(8,128)(2,1)}), bf16[32,2,32,128]{3,2,1,0:T(8,128)(2,1)S(1)}, u32[]{:S(2)}, u32[]{:S(2)}) async-start(bf16[32,2,32,128]{3,2,1,0:T(8,128)(2,1)} %select_multiply_fusion.2), calls=%async_computation.1 | async-start | bytes 1048576 | tf_op jit(solution)/shard_map/while/body/eval_jaxpr/all_to_all | solution.py:60
  160.4 9.5 %all-to-all-done.1 = bf16[32,2,32,128]{3,2,1,0:T(8,128)(2,1)S(1)} async-done(((bf16[32,2,32,128]{3,2,1,0:T(8,128)(2,1)}), bf16[32,2,32,128]{3,2,1,0:T(8,128)(2,1)S(1)}, u32[]{:S(2)}, u32[]{:S(2)}) %all-to-all-start.1) | async-done | bytes 524320 | tf_op jit(solution)/shard_map/while/body/eval_jaxpr/all_to_all | solution.py:60
  170.8 3.5 all-to-all-start
  176.6 15.2 %all-to-all-done = bf16[8,8,32,128]{3,2,1,0:T(8,128)(2,1)S(1)} async-done(((bf16[8,8,32,128]{3,2,1,0:T(8,128)(2,1)}), bf16[8,8,32,128]{3,2,1,0:T(8,128)(2,1)S(1)}, u32[]{:S(2)}, u32[]{:S(2)}) %all-to-all-start) | async-done | bytes 524320 | tf_op jit(solution)/shard_map/while/body/eval_jaxpr/all_to_all | solution.py:40
  192.9 4.4 fusion.40
  200.3 6.3 %all-to-all-start.1 = ((bf16[32,2,32,128]{3,2,1,0:T(8,128)(2,1)}), bf16[32,2,32,128]{3,2,1,0:T(8,128)(2,1)S(1)}, u32[]{:S(2)}, u32[]{:S(2)}) async-start(bf16[32,2,32,128]{3,2,1,0:T(8,128)(2,1)} %select_multiply_fusion.2), calls=%async_computation.1 | async-start | bytes 1048576 | tf_op jit(solution)/shard_map/while/body/eval_jaxpr/all_to_all | solution.py:60
  206.9 9.5 %all-to-all-done.1 = bf16[32,2,32,128]{3,2,1,0:T(8,128)(2,1)S(1)} async-done(((bf16[32,2,32,128]{3,2,1,0:T(8,128)(2,1)}), bf16[32,2,32,128]{3,2,1,0:T(8,128)(2,1)S(1)}, u32[]{:S(2)}, u32[]{:S(2)}) %all-to-all-start.1) | async-done | bytes 524320 | tf_op jit(solution)/shard_map/while/body/eval_jaxpr/all_to_all | solution.py:60
  217.3 3.5 all-to-all-start
  223.0 15.2 %all-to-all-done = bf16[8,8,32,128]{3,2,1,0:T(8,128)(2,1)S(1)} async-done(((bf16[8,8,32,128]{3,2,1,0:T(8,128)(2,1)}), bf16[8,8,32,128]{3,2,1,0:T(8,128)(2,1)S(1)}, u32[]{:S(2)}, u32[]{:S(2)}) %all-to-all-start) | async-done | bytes 524320 | tf_op jit(solution)/shard_map/while/body/eval_jaxpr/all_to_all | solution.py:40
  239.3 4.4 fusion.40
  246.8 6.3 %all-to-all-start.1 = ((bf16[32,2,32,128]{3,2,1,0:T(8,128)(2,1)}), bf16[32,2,32,128]{3,2,1,0:T(8,128)(2,1)S(1)}, u32[]{:S(2)}, u32[]{:S(2)}) async-start(bf16[32,2,32,128]{3,2,1,0:T(8,128)(2,1)} %select_multiply_fusion.2), calls=%async_computation.1 | async-start | bytes 1048576 | tf_op jit(solution)/shard_map/while/body/eval_jaxpr/all_to_all | solution.py:60
  253.3 9.5 %all-to-all-done.1 = bf16[32,2,32,128]{3,2,1,0:T(8,128)(2,1)S(1)} async-done(((bf16[32,2,32,128]{3,2,1,0:T(8,128)(2,1)}), bf16[32,2,32,128]{3,2,1,0:T(8,128)(2,1)S(1)}, u32[]{:S(2)}, u32[]{:S(2)}) %all-to-all-start.1) | async-done | bytes 524320 | tf_op jit(solution)/shard_map/while/body/eval_jaxpr/all_to_all | solution.py:60
  263.7 3.5 all-to-all-start
  269.5 15.2 %all-to-all-done = bf16[8,8,32,128]{3,2,1,0:T(8,128)(2,1)S(1)} async-done(((bf16[8,8,32,128]{3,2,1,0:T(8,128)(2,1)}), bf16[8,8,32,128]{3,2,1,0:T(8,128)(2,1)S(1)}, u32[]{:S(2)}, u32[]{:S(2)}) %all-to-all-start) | async-done | bytes 524320 | tf_op jit(solution)/shard_map/while/body/eval_jaxpr/all_to_all | solution.py:40
  285.7 4.4 fusion.40
  293.2 6.3 %all-to-all-start.1 = ((bf16[32,2,32,128]{3,2,1,0:T(8,128)(2,1)}), bf16[32,2,32,128]{3,2,1,0:T(8,128)(2,1)S(1)}, u32[]{:S(2)}, u32[]{:S(2)}) async-start(bf16[32,2,32,128]{3,2,1,0:T(8,128)(2,1)} %select_multiply_fusion.2), calls=%async_computation.1 | async-start | bytes 1048576 | tf_op jit(solution)/shard_map/while/body/eval_jaxpr/all_to_all | solution.py:60
  299.7 9.5 %all-to-all-done.1 = bf16[32,2,32,128]{3,2,1,0:T(8,128)(2,1)S(1)} async-done(((bf16[32,2,32,128]{3,2,1,0:T(8,128)(2,1)}), bf16[32,2,32,128]{3,2,1,0:T(8,128)(2,1)S(1)}, u32[]{:S(2)}, u32[]{:S(2)}) %all-to-all-start.1) | async-done | bytes 524320 | tf_op jit(solution)/shard_map/while/body/eval_jaxpr/all_to_all | solution.py:60
  310.1 3.5 all-to-all-start
  315.9 15.2 %all-to-all-done = bf16[8,8,32,128]{3,2,1,0:T(8,128)(2,1)S(1)} async-done(((bf16[8,8,32,128]{3,2,1,0:T(8,128)(2,1)}), bf16[8,8,32,128]{3,2,1,0:T(8,128)(2,1)S(1)}, u32[]{:S(2)}, u32[]{:S(2)}) %all-to-all-start) | async-done | bytes 524320 | tf_op jit(solution)/shard_map/while/body/eval_jaxpr/all_to_all | solution.py:40
  332.2 4.4 fusion.40
  339.7 6.3 %all-to-all-start.1 = ((bf16[32,2,32,128]{3,2,1,0:T(8,128)(2,1)}), bf16[32,2,32,128]{3,2,1,0:T(8,128)(2,1)S(1)}, u32[]{:S(2)}, u32[]{:S(2)}) async-start(bf16[32,2,32,128]{3,2,1,0:T(8,128)(2,1)} %select_multiply_fusion.2), calls=%async_computation.1 | async-start | bytes 1048576 | tf_op jit(solution)/shard_map/while/body/eval_jaxpr/all_to_all | solution.py:60
  346.2 9.5 %all-to-all-done.1 = bf16[32,2,32,128]{3,2,1,0:T(8,128)(2,1)S(1)} async-done(((bf16[32,2,32,128]{3,2,1,0:T(8,128)(2,1)}), bf16[32,2,32,128]{3,2,1,0:T(8,128)(2,1)S(1)}, u32[]{:S(2)}, u32[]{:S(2)}) %all-to-all-start.1) | async-done | bytes 524320 | tf_op jit(solution)/shard_map/while/body/eval_jaxpr/all_to_all | solution.py:60
  356.6 3.5 all-to-all-start
  362.4 15.2 %all-to-all-done = bf16[8,8,32,128]{3,2,1,0:T(8,128)(2,1)S(1)} async-done(((bf16[8,8,32,128]{3,2,1,0:T(8,128)(2,1)}), bf16[8,8,32,128]{3,2,1,0:T(8,128)(2,1)S(1)}, u32[]{:S(2)}, u32[]{:S(2)}) %all-to-all-start) | async-done | bytes 524320 | tf_op jit(solution)/shard_map/while/body/eval_jaxpr/all_to_all | solution.py:40
  378.6 4.4 fusion.40
  386.1 6.3 %all-to-all-start.1 = ((bf16[32,2,32,128]{3,2,1,0:T(8,128)(2,1)}), bf16[32,2,32,128]{3,2,1,0:T(8,128)(2,1)S(1)}, u32[]{:S(2)}, u32[]{:S(2)}) async-start(bf16[32,2,32,128]{3,2,1,0:T(8,128)(2,1)} %select_multiply_fusion.2), calls=%async_computation.1 | async-start | bytes 1048576 | tf_op jit(solution)/shard_map/while/body/eval_jaxpr/all_to_all | solution.py:60
  392.6 9.5 %all-to-all-done.1 = bf16[32,2,32,128]{3,2,1,0:T(8,128)(2,1)S(1)} async-done(((bf16[32,2,32,128]{3,2,1,0:T(8,128)(2,1)}), bf16[32,2,32,128]{3,2,1,0:T(8,128)(2,1)S(1)}, u32[]{:S(2)}, u32[]{:S(2)}) %all-to-all-start.1) | async-done | bytes 524320 | tf_op jit(solution)/shard_map/while/body/eval_jaxpr/all_to_all | solution.py:60
  408.8 15.2 %all-to-all-done = bf16[8,8,32,128]{3,2,1,0:T(8,128)(2,1)S(1)} async-done(((bf16[8,8,32,128]{3,2,1,0:T(8,128)(2,1)}), bf16[8,8,32,128]{3,2,1,0:T(8,128)(2,1)S(1)}, u32[]{:S(2)}, u32[]{:S(2)}) %all-to-all-start) | async-done | bytes 524320 | tf_op jit(solution)/shard_map/while/body/eval_jaxpr/all_to_all | solution.py:40
  425.1 4.4 fusion.40
  432.5 6.3 %all-to-all-start.1 = ((bf16[32,2,32,128]{3,2,1,0:T(8,128)(2,1)}), bf16[32,2,32,128]{3,2,1,0:T(8,128)(2,1)S(1)}, u32[]{:S(2)}, u32[]{:S(2)}) async-start(bf16[32,2,32,128]{3,2,1,0:T(8,128)(2,1)} %select_multiply_fusion.2), calls=%async_computation.1 | async-start | bytes 1048576 | tf_op jit(solution)/shard_map/while/body/eval_jaxpr/all_to_all | solution.py:60
  439.1 9.5 %all-to-all-done.1 = bf16[32,2,32,128]{3,2,1,0:T(8,128)(2,1)S(1)} async-done(((bf16[32,2,32,128]{3,2,1,0:T(8,128)(2,1)}), bf16[32,2,32,128]{3,2,1,0:T(8,128)(2,1)S(1)}, u32[]{:S(2)}, u32[]{:S(2)}) %all-to-all-start.1) | async-done | bytes 524320 | tf_op jit(solution)/shard_map/while/body/eval_jaxpr/all_to_all | solution.py:60
  455.3 15.2 %all-to-all-done = bf16[8,8,32,128]{3,2,1,0:T(8,128)(2,1)S(1)} async-done(((bf16[8,8,32,128]{3,2,1,0:T(8,128)(2,1)}), bf16[8,8,32,128]{3,2,1,0:T(8,128)(2,1)S(1)}, u32[]{:S(2)}, u32[]{:S(2)}) %all-to-all-start) | async-done | bytes 524320 | tf_op jit(solution)/shard_map/while/body/eval_jaxpr/all_to_all | solution.py:40
  471.5 4.4 fusion.40
  (423 shorter events, 89.5 us)
Async XLA Ops:
  6.9 9.3 %copy-start.4 = (s32[8,32]{1,0:T(8,128)S(1)}, s32[8,32]{1,0:T(8,128)}, u32[]{:S(2)}) copy-start(s32[8,32]{1,0:T(8,128)} %get-tuple-element.279) | copy-start | bytes 3076 | tf_op jit(solution)/shard_map/while
  7.6 28.4 %copy-start.5 = (f32[8,1,128]{2,0,1:T(8,128)S(1)}, f32[8,1,128]{2,0,1:T(8,128)}, u32[]{:S(2)}) copy-start(f32[8,1,128]{2,0,1:T(8,128)} %get-tuple-element.278) | copy-start | bytes 12292 | tf_op jit(solution)/shard_map/while
  8.6 17.3 %all-to-all-start.1 = ((bf16[32,2,32,128]{3,2,1,0:T(8,128)(2,1)}), bf16[32,2,32,128]{3,2,1,0:T(8,128)(2,1)S(1)}, u32[]{:S(2)}, u32[]{:S(2)}) async-start(bf16[32,2,32,128]{3,2,1,0:T(8,128)(2,1)} %select_multiply_fusion.2), calls=%async_computation.1 | async-start | bytes 1048576 | tf_op jit(solution)/shard_map/while/body/eval_jaxpr/all_to_all | solution.py:60
  26.7 25.8 %all-to-all-start = ((bf16[8,8,32,128]{3,2,1,0:T(8,128)(2,1)}), bf16[8,8,32,128]{3,2,1,0:T(8,128)(2,1)S(1)}, u32[]{:S(2)}, u32[]{:S(2)}) async-start(bf16[8,8,32,128]{3,2,1,0:T(8,128)(2,1)} %stack.4), calls=%async_computation | async-start | bytes 1048576 | tf_op jit(solution)/shard_map/while/body/eval_jaxpr/all_to_all | solution.py:40
  59.4 8.0 %copy-start.4 = (s32[8,32]{1,0:T(8,128)S(1)}, s32[8,32]{1,0:T(8,128)}, u32[]{:S(2)}) copy-start(s32[8,32]{1,0:T(8,128)} %get-tuple-element.279) | copy-start | bytes 3076 | tf_op jit(solution)/shard_map/while
  60.1 22.2 %copy-start.5 = (f32[8,1,128]{2,0,1:T(8,128)S(1)}, f32[8,1,128]{2,0,1:T(8,128)}, u32[]{:S(2)}) copy-start(f32[8,1,128]{2,0,1:T(8,128)} %get-tuple-element.278) | copy-start | bytes 12292 | tf_op jit(solution)/shard_map/while
  61.0 16.1 %all-to-all-start.1 = ((bf16[32,2,32,128]{3,2,1,0:T(8,128)(2,1)}), bf16[32,2,32,128]{3,2,1,0:T(8,128)(2,1)S(1)}, u32[]{:S(2)}, u32[]{:S(2)}) async-start(bf16[32,2,32,128]{3,2,1,0:T(8,128)(2,1)} %select_multiply_fusion.2), calls=%async_computation.1 | async-start | bytes 1048576 | tf_op jit(solution)/shard_map/while/body/eval_jaxpr/all_to_all | solution.py:60
  77.9 21.0 %all-to-all-start = ((bf16[8,8,32,128]{3,2,1,0:T(8,128)(2,1)}), bf16[8,8,32,128]{3,2,1,0:T(8,128)(2,1)S(1)}, u32[]{:S(2)}, u32[]{:S(2)}) async-start(bf16[8,8,32,128]{3,2,1,0:T(8,128)(2,1)} %stack.4), calls=%async_computation | async-start | bytes 1048576 | tf_op jit(solution)/shard_map/while/body/eval_jaxpr/all_to_all | solution.py:40
  105.8 7.9 %copy-start.4 = (s32[8,32]{1,0:T(8,128)S(1)}, s32[8,32]{1,0:T(8,128)}, u32[]{:S(2)}) copy-start(s32[8,32]{1,0:T(8,128)} %get-tuple-element.279) | copy-start | bytes 3076 | tf_op jit(solution)/shard_map/while
  106.5 22.2 %copy-start.5 = (f32[8,1,128]{2,0,1:T(8,128)S(1)}, f32[8,1,128]{2,0,1:T(8,128)}, u32[]{:S(2)}) copy-start(f32[8,1,128]{2,0,1:T(8,128)} %get-tuple-element.278) | copy-start | bytes 12292 | tf_op jit(solution)/shard_map/while
  107.4 16.0 %all-to-all-start.1 = ((bf16[32,2,32,128]{3,2,1,0:T(8,128)(2,1)}), bf16[32,2,32,128]{3,2,1,0:T(8,128)(2,1)S(1)}, u32[]{:S(2)}, u32[]{:S(2)}) async-start(bf16[32,2,32,128]{3,2,1,0:T(8,128)(2,1)} %select_multiply_fusion.2), calls=%async_computation.1 | async-start | bytes 1048576 | tf_op jit(solution)/shard_map/while/body/eval_jaxpr/all_to_all | solution.py:60
  124.4 21.0 %all-to-all-start = ((bf16[8,8,32,128]{3,2,1,0:T(8,128)(2,1)}), bf16[8,8,32,128]{3,2,1,0:T(8,128)(2,1)S(1)}, u32[]{:S(2)}, u32[]{:S(2)}) async-start(bf16[8,8,32,128]{3,2,1,0:T(8,128)(2,1)} %stack.4), calls=%async_computation | async-start | bytes 1048576 | tf_op jit(solution)/shard_map/while/body/eval_jaxpr/all_to_all | solution.py:40
  146.4 4.5 copy-start
  152.3 7.9 %copy-start.4 = (s32[8,32]{1,0:T(8,128)S(1)}, s32[8,32]{1,0:T(8,128)}, u32[]{:S(2)}) copy-start(s32[8,32]{1,0:T(8,128)} %get-tuple-element.279) | copy-start | bytes 3076 | tf_op jit(solution)/shard_map/while
  152.9 22.2 %copy-start.5 = (f32[8,1,128]{2,0,1:T(8,128)S(1)}, f32[8,1,128]{2,0,1:T(8,128)}, u32[]{:S(2)}) copy-start(f32[8,1,128]{2,0,1:T(8,128)} %get-tuple-element.278) | copy-start | bytes 12292 | tf_op jit(solution)/shard_map/while
  153.9 16.1 %all-to-all-start.1 = ((bf16[32,2,32,128]{3,2,1,0:T(8,128)(2,1)}), bf16[32,2,32,128]{3,2,1,0:T(8,128)(2,1)S(1)}, u32[]{:S(2)}, u32[]{:S(2)}) async-start(bf16[32,2,32,128]{3,2,1,0:T(8,128)(2,1)} %select_multiply_fusion.2), calls=%async_computation.1 | async-start | bytes 1048576 | tf_op jit(solution)/shard_map/while/body/eval_jaxpr/all_to_all | solution.py:60
  170.8 21.0 %all-to-all-start = ((bf16[8,8,32,128]{3,2,1,0:T(8,128)(2,1)}), bf16[8,8,32,128]{3,2,1,0:T(8,128)(2,1)S(1)}, u32[]{:S(2)}, u32[]{:S(2)}) async-start(bf16[8,8,32,128]{3,2,1,0:T(8,128)(2,1)} %stack.4), calls=%async_computation | async-start | bytes 1048576 | tf_op jit(solution)/shard_map/while/body/eval_jaxpr/all_to_all | solution.py:40
  192.8 4.5 copy-start
  198.7 7.9 %copy-start.4 = (s32[8,32]{1,0:T(8,128)S(1)}, s32[8,32]{1,0:T(8,128)}, u32[]{:S(2)}) copy-start(s32[8,32]{1,0:T(8,128)} %get-tuple-element.279) | copy-start | bytes 3076 | tf_op jit(solution)/shard_map/while
  199.4 22.2 %copy-start.5 = (f32[8,1,128]{2,0,1:T(8,128)S(1)}, f32[8,1,128]{2,0,1:T(8,128)}, u32[]{:S(2)}) copy-start(f32[8,1,128]{2,0,1:T(8,128)} %get-tuple-element.278) | copy-start | bytes 12292 | tf_op jit(solution)/shard_map/while
  200.3 16.1 %all-to-all-start.1 = ((bf16[32,2,32,128]{3,2,1,0:T(8,128)(2,1)}), bf16[32,2,32,128]{3,2,1,0:T(8,128)(2,1)S(1)}, u32[]{:S(2)}, u32[]{:S(2)}) async-start(bf16[32,2,32,128]{3,2,1,0:T(8,128)(2,1)} %select_multiply_fusion.2), calls=%async_computation.1 | async-start | bytes 1048576 | tf_op jit(solution)/shard_map/while/body/eval_jaxpr/all_to_all | solution.py:60
  217.3 21.0 %all-to-all-start = ((bf16[8,8,32,128]{3,2,1,0:T(8,128)(2,1)}), bf16[8,8,32,128]{3,2,1,0:T(8,128)(2,1)S(1)}, u32[]{:S(2)}, u32[]{:S(2)}) async-start(bf16[8,8,32,128]{3,2,1,0:T(8,128)(2,1)} %stack.4), calls=%async_computation | async-start | bytes 1048576 | tf_op jit(solution)/shard_map/while/body/eval_jaxpr/all_to_all | solution.py:40
  239.3 4.5 copy-start
  245.1 7.9 %copy-start.4 = (s32[8,32]{1,0:T(8,128)S(1)}, s32[8,32]{1,0:T(8,128)}, u32[]{:S(2)}) copy-start(s32[8,32]{1,0:T(8,128)} %get-tuple-element.279) | copy-start | bytes 3076 | tf_op jit(solution)/shard_map/while
  245.8 22.2 %copy-start.5 = (f32[8,1,128]{2,0,1:T(8,128)S(1)}, f32[8,1,128]{2,0,1:T(8,128)}, u32[]{:S(2)}) copy-start(f32[8,1,128]{2,0,1:T(8,128)} %get-tuple-element.278) | copy-start | bytes 12292 | tf_op jit(solution)/shard_map/while
  246.8 16.1 %all-to-all-start.1 = ((bf16[32,2,32,128]{3,2,1,0:T(8,128)(2,1)}), bf16[32,2,32,128]{3,2,1,0:T(8,128)(2,1)S(1)}, u32[]{:S(2)}, u32[]{:S(2)}) async-start(bf16[32,2,32,128]{3,2,1,0:T(8,128)(2,1)} %select_multiply_fusion.2), calls=%async_computation.1 | async-start | bytes 1048576 | tf_op jit(solution)/shard_map/while/body/eval_jaxpr/all_to_all | solution.py:60
  263.7 21.0 %all-to-all-start = ((bf16[8,8,32,128]{3,2,1,0:T(8,128)(2,1)}), bf16[8,8,32,128]{3,2,1,0:T(8,128)(2,1)S(1)}, u32[]{:S(2)}, u32[]{:S(2)}) async-start(bf16[8,8,32,128]{3,2,1,0:T(8,128)(2,1)} %stack.4), calls=%async_computation | async-start | bytes 1048576 | tf_op jit(solution)/shard_map/while/body/eval_jaxpr/all_to_all | solution.py:40
  285.7 4.5 copy-start
  291.6 7.9 %copy-start.4 = (s32[8,32]{1,0:T(8,128)S(1)}, s32[8,32]{1,0:T(8,128)}, u32[]{:S(2)}) copy-start(s32[8,32]{1,0:T(8,128)} %get-tuple-element.279) | copy-start | bytes 3076 | tf_op jit(solution)/shard_map/while
  292.3 22.2 %copy-start.5 = (f32[8,1,128]{2,0,1:T(8,128)S(1)}, f32[8,1,128]{2,0,1:T(8,128)}, u32[]{:S(2)}) copy-start(f32[8,1,128]{2,0,1:T(8,128)} %get-tuple-element.278) | copy-start | bytes 12292 | tf_op jit(solution)/shard_map/while
  293.2 16.1 %all-to-all-start.1 = ((bf16[32,2,32,128]{3,2,1,0:T(8,128)(2,1)}), bf16[32,2,32,128]{3,2,1,0:T(8,128)(2,1)S(1)}, u32[]{:S(2)}, u32[]{:S(2)}) async-start(bf16[32,2,32,128]{3,2,1,0:T(8,128)(2,1)} %select_multiply_fusion.2), calls=%async_computation.1 | async-start | bytes 1048576 | tf_op jit(solution)/shard_map/while/body/eval_jaxpr/all_to_all | solution.py:60
  310.1 21.0 %all-to-all-start = ((bf16[8,8,32,128]{3,2,1,0:T(8,128)(2,1)}), bf16[8,8,32,128]{3,2,1,0:T(8,128)(2,1)S(1)}, u32[]{:S(2)}, u32[]{:S(2)}) async-start(bf16[8,8,32,128]{3,2,1,0:T(8,128)(2,1)} %stack.4), calls=%async_computation | async-start | bytes 1048576 | tf_op jit(solution)/shard_map/while/body/eval_jaxpr/all_to_all | solution.py:40
  332.2 4.5 copy-start
  338.0 7.9 %copy-start.4 = (s32[8,32]{1,0:T(8,128)S(1)}, s32[8,32]{1,0:T(8,128)}, u32[]{:S(2)}) copy-start(s32[8,32]{1,0:T(8,128)} %get-tuple-element.279) | copy-start | bytes 3076 | tf_op jit(solution)/shard_map/while
  338.7 22.2 %copy-start.5 = (f32[8,1,128]{2,0,1:T(8,128)S(1)}, f32[8,1,128]{2,0,1:T(8,128)}, u32[]{:S(2)}) copy-start(f32[8,1,128]{2,0,1:T(8,128)} %get-tuple-element.278) | copy-start | bytes 12292 | tf_op jit(solution)/shard_map/while
  339.7 16.1 %all-to-all-start.1 = ((bf16[32,2,32,128]{3,2,1,0:T(8,128)(2,1)}), bf16[32,2,32,128]{3,2,1,0:T(8,128)(2,1)S(1)}, u32[]{:S(2)}, u32[]{:S(2)}) async-start(bf16[32,2,32,128]{3,2,1,0:T(8,128)(2,1)} %select_multiply_fusion.2), calls=%async_computation.1 | async-start | bytes 1048576 | tf_op jit(solution)/shard_map/while/body/eval_jaxpr/all_to_all | solution.py:60
  356.6 21.0 %all-to-all-start = ((bf16[8,8,32,128]{3,2,1,0:T(8,128)(2,1)}), bf16[8,8,32,128]{3,2,1,0:T(8,128)(2,1)S(1)}, u32[]{:S(2)}, u32[]{:S(2)}) async-start(bf16[8,8,32,128]{3,2,1,0:T(8,128)(2,1)} %stack.4), calls=%async_computation | async-start | bytes 1048576 | tf_op jit(solution)/shard_map/while/body/eval_jaxpr/all_to_all | solution.py:40
  378.6 4.5 copy-start
  384.5 7.9 %copy-start.4 = (s32[8,32]{1,0:T(8,128)S(1)}, s32[8,32]{1,0:T(8,128)}, u32[]{:S(2)}) copy-start(s32[8,32]{1,0:T(8,128)} %get-tuple-element.279) | copy-start | bytes 3076 | tf_op jit(solution)/shard_map/while
  385.2 22.2 %copy-start.5 = (f32[8,1,128]{2,0,1:T(8,128)S(1)}, f32[8,1,128]{2,0,1:T(8,128)}, u32[]{:S(2)}) copy-start(f32[8,1,128]{2,0,1:T(8,128)} %get-tuple-element.278) | copy-start | bytes 12292 | tf_op jit(solution)/shard_map/while
  386.1 16.1 %all-to-all-start.1 = ((bf16[32,2,32,128]{3,2,1,0:T(8,128)(2,1)}), bf16[32,2,32,128]{3,2,1,0:T(8,128)(2,1)S(1)}, u32[]{:S(2)}, u32[]{:S(2)}) async-start(bf16[32,2,32,128]{3,2,1,0:T(8,128)(2,1)} %select_multiply_fusion.2), calls=%async_computation.1 | async-start | bytes 1048576 | tf_op jit(solution)/shard_map/while/body/eval_jaxpr/all_to_all | solution.py:60
  403.0 21.0 %all-to-all-start = ((bf16[8,8,32,128]{3,2,1,0:T(8,128)(2,1)}), bf16[8,8,32,128]{3,2,1,0:T(8,128)(2,1)S(1)}, u32[]{:S(2)}, u32[]{:S(2)}) async-start(bf16[8,8,32,128]{3,2,1,0:T(8,128)(2,1)} %stack.4), calls=%async_computation | async-start | bytes 1048576 | tf_op jit(solution)/shard_map/while/body/eval_jaxpr/all_to_all | solution.py:40
  425.0 4.5 copy-start
  430.9 7.9 %copy-start.4 = (s32[8,32]{1,0:T(8,128)S(1)}, s32[8,32]{1,0:T(8,128)}, u32[]{:S(2)}) copy-start(s32[8,32]{1,0:T(8,128)} %get-tuple-element.279) | copy-start | bytes 3076 | tf_op jit(solution)/shard_map/while
  431.6 22.2 %copy-start.5 = (f32[8,1,128]{2,0,1:T(8,128)S(1)}, f32[8,1,128]{2,0,1:T(8,128)}, u32[]{:S(2)}) copy-start(f32[8,1,128]{2,0,1:T(8,128)} %get-tuple-element.278) | copy-start | bytes 12292 | tf_op jit(solution)/shard_map/while
  432.5 16.1 %all-to-all-start.1 = ((bf16[32,2,32,128]{3,2,1,0:T(8,128)(2,1)}), bf16[32,2,32,128]{3,2,1,0:T(8,128)(2,1)S(1)}, u32[]{:S(2)}, u32[]{:S(2)}) async-start(bf16[32,2,32,128]{3,2,1,0:T(8,128)(2,1)} %select_multiply_fusion.2), calls=%async_computation.1 | async-start | bytes 1048576 | tf_op jit(solution)/shard_map/while/body/eval_jaxpr/all_to_all | solution.py:60
  449.5 21.0 %all-to-all-start = ((bf16[8,8,32,128]{3,2,1,0:T(8,128)(2,1)}), bf16[8,8,32,128]{3,2,1,0:T(8,128)(2,1)S(1)}, u32[]{:S(2)}, u32[]{:S(2)}) async-start(bf16[8,8,32,128]{3,2,1,0:T(8,128)(2,1)} %stack.4), calls=%async_computation | async-start | bytes 1048576 | tf_op jit(solution)/shard_map/while/body/eval_jaxpr/all_to_all | solution.py:40
  471.5 4.5 copy-start
  (32 other events, 105.3 us)
